TPU v7x, 256 devices: a whole 4x4x8 slice. The times are simulated.
256 devices in a mesh: dp: 32 (over y_hi, z, core), fsdp: 8 (over x, y_lo).
Axes of the slice: x: 4, y: 4 (y_hi: 2, y_lo: 2; y = y_hi * 2 + y_lo), z: 8, core: 2. Of those that a mesh axis runs over, the one named last changes fastest.
Arguments:
- tokens: bfloat16 [4096, 4096], P(('fsdp', 'dp')), may hold values from -6 to 6
- upstream: bfloat16 [4096, 4096], P(('fsdp', 'dp')), may hold values from -0.375 to 0.375
- old_master: float32 [4096, 3, 5632], P(('fsdp', 'dp')), may hold values from -0.09375 to 0.09375
- old_first: float32 [4096, 3, 5632], P(('fsdp', 'dp')), may hold values from -3 to 3
- old_second: float32 [4096, 3, 5632], P(('fsdp', 'dp')), may hold values from 0.01 to 4
- grown_master: float32 [4096, 3, 2560], P(('fsdp', 'dp')), may hold values from -0.09375 to 0.09375
- grown_first: float32 [4096, 3, 2560], P(('fsdp', 'dp')), may hold values from -3 to 3
- grown_second: float32 [4096, 3, 2560], P(('fsdp', 'dp')), may hold values from 0.01 to 4
- grow_mask: float32 [2560], replicated, may hold values from 0.1 to 1
Outputs:
- layer_output: bfloat16 [4096, 4096], P(('fsdp', 'dp'))
- new_master: float32 [4096, 3, 8192], P('fsdp', None, 'dp')
- new_first: float32 [4096, 3, 8192], P('fsdp', None, 'dp')
- new_second: float32 [4096, 3, 8192], P('fsdp', None, 'dp')
All inputs are finite; a program needn't handle non-finite values.
Results may differ from a plain program's by a relative error of at most 0.019.
Values may be sent and summed in bfloat16 or wider, within the bound.
A program may use at most 128 MiB of HBM per device.

v0:
```python
import jax
import jax.numpy as jnp
from jax import lax
from jax.sharding import PartitionSpec as P

STEP = 1000


beta_first = 0.9
beta_second = 0.999
adam_epsilon = 1e-08
learn_rate = 0.001
weight_decay = 0.1


def sent_together(arrays, axis, dim, along):
    both = jnp.concatenate(arrays, axis=along)
    filled, at, gathered = (lax.all_gather(both, axis, axis=dim, tiled=True), 0, [])
    for a in arrays:
        gathered.append(lax.slice_in_dim(filled, at, at + a.shape[along], axis=along))
        at += a.shape[along]
    return tuple(gathered)


def split_up(array, dim, size):
    lengths = array.shape
    parts = array.reshape(*lengths[:dim], size, lengths[dim] // size, *lengths[dim + 1 :])
    return jnp.moveaxis(parts, dim, 0)


def sent_and_summed(array, axis, dim):
    parts = split_up(array, dim, lax.axis_size(axis))
    arrived = lax.all_to_all(parts, axis, split_axis=0, concat_axis=0, tiled=True)
    return arrived.astype(jnp.float32).sum(axis=0)


def in_one_piece(arrays, axis, split_dim, concat_dim, along):
    both = jnp.concatenate(arrays, axis=along)
    filled, at, gathered = (
        lax.all_to_all(both, axis, split_axis=split_dim, concat_axis=concat_dim, tiled=True),
        0,
        [],
    )
    for a in arrays:
        gathered.append(lax.slice_in_dim(filled, at, at + a.shape[along], axis=along))
        at += a.shape[along]
    return tuple(gathered)


def contract_rows(left_part, right_part):
    return lax.dot_general(
        left_part, right_part, (((0,), (0,)), ((), ())), preferred_element_type=jnp.float32
    )


def contract_last(left_part, right_part):
    return lax.dot_general(
        left_part, right_part, (((1,), (1,)), ((), ())), preferred_element_type=jnp.float32
    )


def adam_update(master, first_moment, second_moment, gradients):
    new_first = beta_first * first_moment + (1.0 - beta_first) * gradients
    new_second = beta_second * second_moment + (1.0 - beta_second) * gradients * gradients
    first_hat = new_first / (1.0 - beta_first**STEP)
    second_hat = new_second / (1.0 - beta_second**STEP)
    new_master = master - learn_rate * (
        first_hat / (jnp.sqrt(second_hat) + adam_epsilon) + weight_decay * master
    )
    return (new_master, new_first, new_second)


def local(
    tokens,
    upstream,
    old_master,
    old_first,
    old_second,
    grown_master,
    grown_first,
    grown_second,
    grow_mask,
):
    new_width = old_master.shape[2] + grown_master.shape[2]
    block_width = new_width // lax.axis_size("dp")
    master_all = jnp.concatenate([old_master, grown_master], axis=2)
    first_all = jnp.concatenate([old_first, grown_first], axis=2)
    second_all = jnp.concatenate([old_second, grown_second], axis=2)
    master = lax.all_to_all(
        master_all.astype(jnp.bfloat16), "dp", split_axis=2, concat_axis=0, tiled=True
    ).astype(master_all.dtype)
    weights = lax.all_gather(master.astype(jnp.bfloat16), "fsdp", axis=0, tiled=True)
    rows_in, rows_back = sent_together((tokens, upstream), "dp", 0, 1)
    all_scales = jnp.concatenate([jnp.ones((old_master.shape[2],), jnp.float32), grow_mask])
    scales = lax.dynamic_slice_in_dim(all_scales, lax.axis_index("dp") * block_width, block_width)
    model_width = weights.shape[0]
    paired = weights[:, :2, :].reshape(model_width, 2 * block_width)
    down_weights = weights[:, 2, :]
    projected = jnp.dot(rows_in, paired, preferred_element_type=jnp.float32)
    gate_value = projected[:, :block_width]
    up_value = projected[:, block_width:]
    sigmoid_gate = jax.nn.sigmoid(gate_value)
    activated = gate_value * sigmoid_gate
    hidden = (activated * up_value * scales).astype(jnp.bfloat16)
    summed = lax.psum_scatter(
        contract_last(hidden, down_weights).astype(jnp.bfloat16),
        "dp",
        scatter_dimension=0,
        tiled=True,
    )
    back_hidden = jnp.dot(rows_back, down_weights, preferred_element_type=jnp.float32) * scales
    own_rows = master.shape[0]
    down_grad = sent_and_summed(contract_rows(rows_back, hidden).astype(jnp.bfloat16), "fsdp", 0)
    gate_back = (
        back_hidden * up_value * sigmoid_gate * (1.0 + gate_value * (1.0 - sigmoid_gate))
    ).astype(jnp.bfloat16)
    up_back = (back_hidden * activated).astype(jnp.bfloat16)
    inner_back = jnp.concatenate([gate_back, up_back], axis=1)
    inner_grad = sent_and_summed(contract_rows(rows_in, inner_back).astype(jnp.bfloat16), "fsdp", 0)
    gradients = jnp.concatenate(
        [inner_grad.reshape(own_rows, 2, block_width), down_grad[:, None, :]], axis=1
    )
    first_moment, second_moment = tuple(
        (
            part.astype(jnp.float32)
            for part in in_one_piece(
                (first_all.astype(jnp.bfloat16), second_all.astype(jnp.bfloat16)), "dp", 2, 0, 1
            )
        )
    )
    new_master, new_first, new_second = adam_update(master, first_moment, second_moment, gradients)
    return (summed, new_master, new_first, new_second)


def solution(mesh):
    in_specs = (
        P(("fsdp", "dp"), None),
        P(("fsdp", "dp"), None),
        P(("fsdp", "dp"), None, None),
        P(("fsdp", "dp"), None, None),
        P(("fsdp", "dp"), None, None),
        P(("fsdp", "dp"), None, None),
        P(("fsdp", "dp"), None, None),
        P(("fsdp", "dp"), None, None),
        P(),
    )
    out_specs = (
        P(("fsdp", "dp"), None),
        P("fsdp", None, "dp"),
        P("fsdp", None, "dp"),
        P("fsdp", None, "dp"),
    )
    return jax.shard_map(local, mesh=mesh, in_specs=in_specs, out_specs=out_specs, check_vma=False)
```

profile of v0, /device:TPU:1, one launch (start us, length us, event | category | flops | bytes accessed | tf_op | source)
XLA Modules:
  0.0 512.7 jit_solution(11075435288912256371)
XLA Ops:
  9.6 8.3 %copy.39 = bf16[16,3,8192]{0,1,2:T(4,128)(2,1)} copy(bf16[16,3,8192]{2,0,1:T(8,128)(2,1)S(1)} %pad_maximum_fusion.1) | data formatting | bytes 1572864 | tf_op jit(solution)/shard_map/concatenate | solution.py:86
  17.9 12.8 %reshape.25 = bf16[32,2,6144]{2,1,0:T(2,128)(2,1)S(1)} reshape(bf16[8192,3,16]{2,1,0:T(4,128)(2,1)} %bitcast.33) | data formatting | bytes 1572864
  30.7 35.3 %all_to_all.46 = bf16[32,2,6144]{2,1,0:T(2,128)(2,1)S(1)} all-to-all(bf16[32,2,6144]{2,1,0:T(2,128)(2,1)S(1)} %reshape.25), channel_id=1, replica_groups=mesh['dp'=32,'fsdp'=8] {'dp'}, dimensions={0} | all-to-all | bytes 1572864 | tf_op jit(solution)/shard_map/all_to_all | solution.py:89
  66.0 10.7 %reshape.26 = bf16[8192,3,16]{2,1,0:T(4,128)(2,1)} reshape(bf16[32,2,6144]{2,1,0:T(2,128)(2,1)S(1)} %all_to_all.46) | data formatting | bytes 1572864
  76.8 10.9 %copy.49 = bf16[16,3,32,256]{3,0,2,1:T(8,128)(2,1)} copy(bf16[16,3,32,256]{0,1,3,2:T(4,128)(2,1)} %bitcast.34) | data formatting | bytes 1572864 | tf_op jit(solution)/shard_map/all_to_all | solution.py:89
  89.7 13.0 %copy.43 = bf16[16,6,8192]{0,1,2:T(8,128)(2,1)} copy(bf16[16,6,8192]{2,0,1:T(8,128)(2,1)S(1)} %maximum_maximum_fusion) | data formatting | bytes 3145728 | tf_op jit(solution)/shard_map/concatenate | solution.py:38
  102.7 18.8 %reshape.27 = bf16[32,2,12288]{2,1,0:T(2,128)(2,1)} reshape(bf16[8192,6,16]{2,1,0:T(8,128)(2,1)} %bitcast.31) | data formatting | bytes 3145728
  121.5 6.0 %all-to-all-start.1 = ((bf16[32,2,12288]{2,1,0:T(2,128)(2,1)}), bf16[32,2,12288]{2,1,0:T(2,128)(2,1)S(1)}, u32[]{:S(2)}, u32[]{:S(2)}) async-start(bf16[32,2,12288]{2,1,0:T(2,128)(2,1)} %reshape.27), calls=%async_computation.2 | async-start | bytes 3145728 | tf_op jit(solution)/shard_map/all_to_all | solution.py:40
  127.6 105.2 %all-gather.5.cloned.1.call-done = bf16[4096,3,256]{2,0,1:T(8,128)(2,1)} async-done(((bf16[512,3,256]{2,0,1:T(8,128)(2,1)}), bf16[4096,3,256]{2,0,1:T(8,128)(2,1)}) %all-gather.5.cloned.1.call-update) | async-done | bytes 6291472 | tf_op jit(solution)/shard_map/all_gather | solution.py:92
  232.8 4.4 slice.33
  237.2 6.5 %copy.42 = bf16[4096,2,256]{0,2,1:T(8,128)(2,1)} copy(bf16[4096,2,256]{2,0,1:T(8,128)(2,1)} %slice.33) | data formatting | bytes 8388608 | tf_op jit(solution)/shard_map/slice | solution.py:97
  243.7 95.7 %all-gather.3.cloned.1.call-done = bf16[512,8192]{1,0:T(8,128)(2,1)} async-done(((bf16[16,8192]{1,0:T(8,128)(2,1)}), bf16[512,8192]{1,0:T(8,128)(2,1)}) %all-gather.3.cloned.1.call-update) | async-done | bytes 8388624 | tf_op jit(solution)/shard_map/all_gather | solution.py:18
  339.3 6.0 %fusion.4 = f32[512,512]{0,1:T(8,128)S(1)} fusion(bf16[4096,512]{0,1:T(8,128)(2,1)} %bitcast.38, bf16[512,8192]{1,0:T(8,128)(2,1)} %all-gather.3.cloned.1.call-done), kind=kOutput, calls=%fused_computation.9 | convolution fusion | flops 2147483648 | bytes 9437184 | tf_op jit(solution)/shard_map/dot_general | solution.py:99
  345.3 3.1 multiply_convert_fusion.1
  352.3 4.0 all-to-all-start.3
  356.5 4.8 convolution_convert_fusion
  361.3 6.6 %convolution_convert_fusion.1 = bf16[4096,512]{1,0:T(8,128)(2,1)} fusion(bf16[512,8192]{1,0:T(8,128)(2,1)} %all-gather.3.cloned.1.call-done, bf16[512,256]{0,1:T(8,128)(2,1)S(1)} %get-tuple-element.12, bf16[512,256]{0,1:T(8,128)(2,1)S(1)} %get-tuple-element.11), kind=kOutput, calls=%fused_computation.2 | convolution fusion | flops 2150629376 | bytes 8912896 | tf_op jit(solution)/shard_map/dot_general | solution.py:51
  367.9 19.3 %all-to-all-done.3 = bf16[8,512,256]{2,1,0:T(8,128)(2,1)S(1)} async-done(((bf16[8,512,256]{2,1,0:T(8,128)(2,1)}), bf16[8,512,256]{2,1,0:T(8,128)(2,1)S(1)}, u32[]{:S(2)}, u32[]{:S(2)}) %all-to-all-start.3) | async-done | bytes 2097184 | tf_op jit(solution)/shard_map/all_to_all | solution.py:33
  387.2 4.6 all-to-all-start.2
  391.8 18.0 %reshape.28 = bf16[8192,6,16]{2,1,0:T(8,128)(2,1)} reshape(bf16[32,2,12288]{2,1,0:T(2,128)(2,1)} %copy-done.1) | data formatting | bytes 3145728
  409.8 14.9 %copy.45 = bf16[32,16,6,256]{3,1,0,2:T(8,128)(2,1)} copy(bf16[32,16,6,256]{1,2,3,0:T(8,128)(2,1)} %bitcast.32) | data formatting | bytes 3145728 | tf_op jit(solution)/shard_map/all_to_all | solution.py:40
  425.9 24.6 %all-to-all-done.2 = bf16[8,512,512]{2,1,0:T(8,128)(2,1)} async-done(((bf16[8,512,512]{2,1,0:T(8,128)(2,1)}), bf16[8,512,512]{2,1,0:T(8,128)(2,1)}, u32[]{:S(2)}, u32[]{:S(2)}) %all-to-all-start.2) | async-done | bytes 4194336 | tf_op jit(solution)/shard_map/all_to_all | solution.py:33
  456.3 4.1 convert_subtract_fusion
  460.4 45.9 %reduce-scatter.2.cloned.1.call-done = bf16[16,4096]{1,0:T(8,128)(2,1)} async-done(((bf16[512,4096]{1,0:T(8,128)(2,1)}), bf16[16,4096]{1,0:T(8,128)(2,1)}) %reduce-scatter.2.cloned.1.call-update) | async-done | bytes 131088 | tf_op jit(solution)/shard_map/reduce_scatter | solution.py:105
  (44 shorter events, 15.4 us)
Async XLA Ops:
  7.2 225.6 %all-gather.5.cloned.1.call-start = ((), (), s32[]{:S(2)}) async-start(), calls=%async_computation.6 | async-start | bytes 7077888 | tf_op jit(solution)/shard_map/all_gather | solution.py:92
  76.8 11.0 %copy-start.7 = (bf16[16,4096]{1,0:T(8,128)(2,1)S(1)}, bf16[16,4096]{1,0:T(8,128)(2,1)}, u32[]{:S(2)}) copy-start(bf16[16,4096]{1,0:T(8,128)(2,1)} %param.10) | copy-start | bytes 393220
  76.8 11.0 %copy-start.8 = (bf16[16,4096]{1,0:T(8,128)(2,1)S(1)}, bf16[16,4096]{1,0:T(8,128)(2,1)}, u32[]{:S(2)}) copy-start(bf16[16,4096]{1,0:T(8,128)(2,1)} %param.9) | copy-start | bytes 393220
  76.8 11.8 %copy-start.5 = (f32[16,3,2560]{2,0,1:T(8,128)S(1)}, f32[16,3,2560]{2,0,1:T(8,128)}, u32[]{:S(2)}) copy-start(f32[16,3,2560]{2,0,1:T(8,128)} %param.16) | copy-start | bytes 1474564
  87.7 1.3 copy-start.3
  87.7 1.4 copy-start.6
  87.7 1.8 copy-start.4
  87.7 251.6 %all-gather.3.cloned.1.call-start = ((), (), s32[]{:S(2)}) async-start(), calls=%async_computation.5 | async-start | bytes 8650752 | tf_op jit(solution)/shard_map/all_gather | solution.py:18
  121.5 6.0 %copy-start.9 = (f32[2560]{0:T(1024)S(1)}, f32[2560]{0:T(1024)}, u32[]{:S(2)}) copy-start(f32[2560]{0:T(1024)} %param.17) | copy-start | bytes 30724
  121.5 229.6 %all-to-all-start.1 = ((bf16[32,2,12288]{2,1,0:T(2,128)(2,1)}), bf16[32,2,12288]{2,1,0:T(2,128)(2,1)S(1)}, u32[]{:S(2)}, u32[]{:S(2)}) async-start(bf16[32,2,12288]{2,1,0:T(2,128)(2,1)} %reshape.27), calls=%async_computation.2 | async-start | bytes 3145728 | tf_op jit(solution)/shard_map/all_to_all | solution.py:40
  339.3 6.0 %copy-start.10 = (bf16[512,8192]{1,0:T(8,128)(2,1)S(1)}, bf16[512,8192]{1,0:T(8,128)(2,1)}, u32[]{:S(2)}) copy-start(bf16[512,8192]{1,0:T(8,128)(2,1)} %all-gather.3.cloned.1.call-done) | copy-start | bytes 25165828
  351.1 1.1 copy-start.1
  352.3 35.0 %all-to-all-start.3 = ((bf16[8,512,256]{2,1,0:T(8,128)(2,1)}), bf16[8,512,256]{2,1,0:T(8,128)(2,1)S(1)}, u32[]{:S(2)}, u32[]{:S(2)}) async-start(bf16[8,512,256]{2,1,0:T(8,128)(2,1)} %bitcast.41), calls=%async_computation.4 | async-start | bytes 4194304 | tf_op jit(solution)/shard_map/all_to_all | solution.py:33
  356.2 150.0 %reduce-scatter.2.cloned.1.call-start = ((), (), s32[]{:S(2)}) async-start(), calls=%async_computation.7 | async-start | bytes 4325376 | tf_op jit(solution)/shard_map/reduce_scatter | solution.py:105
  387.2 63.3 %all-to-all-start.2 = ((bf16[8,512,512]{2,1,0:T(8,128)(2,1)}), bf16[8,512,512]{2,1,0:T(8,128)(2,1)}, u32[]{:S(2)}, u32[]{:S(2)}) async-start(bf16[8,512,512]{2,1,0:T(8,128)(2,1)} %bitcast.37), calls=%async_computation.3 | async-start | bytes 8388608 | tf_op jit(solution)/shard_map/all_to_all | solution.py:33
  453.4 2.9 copy-start
  453.4 2.9 copy-start.2
Sparse Core Ops, SparseCore 0:
  87.8 144.9 all-gather.4
  236.1 103.1 all-gather.2
  361.8 144.3 reduce-scatter.1
where the time goes:
time: 520 us; the launch traced here: 513 us
  waiting for transfers between devices  291 us (56%)
  local copies, waits for them, and re-layouts  123 us (24%)
  blocking collectives  35.3 us (7%)
  matrix products  23.2 us (4%)
  starting transfers between devices  14.9 us (3%)
  between operations  13.9 us (3%)
  other arithmetic  11.5 us (2%)
    all_gather x1, waiting for transfers between devices, local(): lax.all_gather(master.astype(jnp.bfloat16), 'fsdp', axis=0, tiled=True)  105 us
    all_gather x1, waiting for transfers between devices, sent_together(): lax.all_gather(both, axis, axis=dim, tiled=True)  95.7 us
    unnamed x26, local copies, waits for them, and re-layouts  62.3 us
    reduce_scatter x1, waiting for transfers between devices, local(): lax.psum_scatter(contract_last(hidden, down_weights).astype(jnp.bfloat16)...  45.9 us
    all_to_all x2, waiting for transfers between devices, sent_and_summed(): lax.all_to_all(parts, axis, split_axis=0, concat_axis=0, tiled=True)  43.9 us
    all_to_all x1, blocking collectives, local(): lax.all_to_all(master_all.astype(jnp.bfloat16), 'dp', split_axis=2, conca...  35.3 us
    all_to_all x1, local copies, waits for them, and re-layouts, in_one_piece(): lax.all_to_all(both, axis, split_axis=split_dim, concat_axis=concat_dim,...  14.9 us
    concatenate x1, local copies, waits for them, and re-layouts, in_one_piece(): both = jnp.concatenate(arrays, axis=along)  13 us
  transfers between devices with their start and end apart: 6, of which 5 were waited for; matrix products, arithmetic and copies ran while one was open for 22% of the time, Pallas kernels for 0%

commit v1 on v0

v1 whole, which is shorter than its diff:
```python
import functools

import jax
import jax.numpy as jnp
from jax import lax
from jax.experimental import pallas as pl
from jax.experimental.pallas import tpu as pltpu
from jax.sharding import PartitionSpec as P

STEP = 1000

beta_first = 0.9
beta_second = 0.999
adam_epsilon = 1e-08
learn_rate = 0.001
weight_decay = 0.1

BF = jnp.bfloat16
F32 = jnp.float32
MESH = pl.DeviceIdType.MESH

NX, NZ, NDP = 4, 8, 32
PLACE = {k: i for i, k in enumerate((0, 1, 7, 2, 6, 3, 5, 4))}


def adam_update(master, first_moment, second_moment, gradients):
    new_first = beta_first * first_moment + (1.0 - beta_first) * gradients
    new_second = beta_second * second_moment + (1.0 - beta_second) * gradients * gradients
    first_hat = new_first / (1.0 - beta_first**STEP)
    second_hat = new_second / (1.0 - beta_second**STEP)
    new_master = master - learn_rate * (
        first_hat / (jnp.sqrt(second_hat) + adam_epsilon) + weight_decay * master
    )
    return (new_master, new_first, new_second)


def step_kernel(
    tok_hbm,
    ups_hbm,
    om_hbm,
    of_hbm,
    os_hbm,
    gm_hbm,
    gf_hbm,
    gs_hbm,
    mask_ref,
    out_ref,
    grad_ref,
    mom_hbm,
    mas_hbm,
    mf,
    momf,
    stage_w,
    stage_m,
    W,
    T,
    acc,
    H,
    XT,
    G,
    R1,
    R2m,
    R2p,
    RY,
    RYF,
    O,
    RC,
    PT,
    RZp,
    RZm,
    RYH,
    load_sems,
    send_sems,
    a_send,
    a_recv,
    m_send,
    m_recv,
    own_sems,
    tz_recv,
    tc_recv,
    ty_recv,
    w_recv,
    r1_recv,
    r2m_recv,
    r2p_recv,
    ry_recv,
    ryf_recv,
    rc_recv,
    rzp_recv,
    rzm_recv,
    ryh_recv,
):
    f = lax.axis_index("fsdp")
    d = lax.axis_index("dp")
    x, yl = lax.div(f, 2), lax.rem(f, 2)
    yh, z, c = lax.div(d, 16), lax.rem(lax.div(d, 2), NZ), lax.rem(d, 2)

    def fs(dx, du):
        ylu = yl if du == 0 else 1 - yl
        return lax.rem(x + dx, NX) * 2 + ylu

    def dpi(dz, du, dv):
        yhu = yh if du == 0 else 1 - yh
        cv = c if dv == 0 else 1 - c
        return (yhu * NZ + lax.rem(z + dz, NZ)) * 2 + cv

    XP, XM, YP = {"fsdp": fs(1, 0)}, {"fsdp": fs(3, 0)}, {"fsdp": fs(0, 1)}
    ZP, ZM = {"dp": dpi(1, 0, 0)}, {"dp": dpi(7, 0, 0)}
    YH, CP = {"dp": dpi(0, 1, 0)}, {"dp": dpi(0, 0, 1)}

    sent = []

    def send(src, dst, rsem, dev):
        copy = pltpu.make_async_remote_copy(
            src_ref=src,
            dst_ref=dst,
            send_sem=send_sems.at[len(sent)],
            recv_sem=rsem,
            device_id=dev,
            device_id_type=MESH,
        )
        copy.start()
        sent.append(copy)

    def arrived(dst, rsem):
        pltpu.make_async_copy(dst, dst, rsem).wait()

    loads = []

    def load(src, dst):
        copy = pltpu.make_async_copy(src, dst, load_sems.at[len(loads)])
        copy.start()
        loads.append(copy)
        return copy

    n_old = om_hbm.shape[2]
    n_new = gm_hbm.shape[2]
    load_w = [
        (
            load(om_hbm.at[p], mf.at[p, :, pl.ds(0, n_old)]),
            load(gm_hbm.at[p], mf.at[p, :, pl.ds(n_old, n_new)]),
        )
        for p in range(3)
    ]

    def row(k, u, v):
        at = PLACE[k]
        return (at // 4) * 256 + v * 128 + ((at % 4) * 2 + u) * 16

    def blk(k, u, v):
        return T.at[:, pl.ds(row(k, u, v), 16), :]

    load_t = [
        load(tok_hbm, T.at[0, pl.ds(row(0, 0, 0), 16), :]),
        load(ups_hbm, T.at[1, pl.ds(row(0, 0, 0), 16), :]),
    ]
    load_m = [
        load(of_hbm, momf.at[pl.ds(0, 3), :, pl.ds(0, n_old)]),
        load(gf_hbm, momf.at[pl.ds(0, 3), :, pl.ds(n_old, n_new)]),
        load(os_hbm, momf.at[pl.ds(3, 3), :, pl.ds(0, n_old)]),
        load(gs_hbm, momf.at[pl.ds(3, 3), :, pl.ds(n_old, n_new)]),
    ]

    def other(i):
        half = lax.div(i + 1, 2)
        turn = 1 - 2 * lax.rem(i + 1, 2)
        return lax.rem(d + NDP + turn * half, NDP)

    barrier = pltpu.get_barrier_semaphore()

    def greet(i, carry):
        pl.semaphore_signal(
            barrier, inc=1, device_id={"dp": other(i)}, device_id_type=MESH
        )
        return carry

    lax.fori_loop(1, NDP, greet, 0)
    for dev in (XP, XM, YP):
        pl.semaphore_signal(barrier, inc=1, device_id=dev, device_id_type=MESH)

    def wrow(fi, lo, n):
        return pl.ds(pl.multiple_of(fi * 512 + lo, 16), n)

    def mine16(lo):
        return pl.ds(pl.multiple_of(lo + d * 16, 16), 16)

    for p in range(3):
        for copy in load_w[p]:
            copy.wait()
        for j in range(NDP):
            stage_w[p, j] = mf[p, :, j * 256 : (j + 1) * 256].astype(BF)
        W[p, mine16(f * 512), :] = stage_w[p, d]
        if p == 0:
            pl.semaphore_wait(barrier, NDP - 1 + 3)

        def give(i, carry, p=p):
            to = other(i)
            pltpu.make_async_remote_copy(
                src_ref=stage_w.at[p, to],
                dst_ref=W.at[p, mine16(f * 512), :],
                send_sem=a_send.at[p],
                recv_sem=a_recv.at[p],
                device_id={"dp": to},
                device_id_type=MESH,
            ).start()
            return carry

        lax.fori_loop(1, NDP, give, 0)

    def core_send(k, u):
        send(blk(k, u, 0), blk(k, u, 1), tc_recv.at[k, u], CP)

    def ring_up(s, u):
        a, b = (8 - s) % 8, 7 - s
        if b == 4:
            send(
                T.at[0, pl.ds(row(a, u, 0), 16), :],
                T.at[0, pl.ds(row(b, u, 0), 16), :],
                tz_recv.at[4, u],
                ZP,
            )
        else:
            send(blk(a, u, 0), blk(b, u, 0), tz_recv.at[b, u], ZP)

    def ring_down(s, u):
        a, b = s, s + 1
        if b == 4:
            send(
                T.at[1, pl.ds(row(a, u, 0), 16), :],
                T.at[1, pl.ds(row(b, u, 0), 16), :],
                tz_recv.at[8, u],
                ZM,
            )
        else:
            send(blk(a, u, 0), blk(b, u, 0), tz_recv.at[b, u], ZM)

    def ring_step(s, u):
        up, down = (8 - s) % 8, s
        arrived(blk(up, u, 0), tz_recv.at[up, u])
        ring_up(s, u)
        arrived(blk(down, u, 0), tz_recv.at[down, u])
        ring_down(s, u)
        core_send(up, u)
        core_send(down, u)

    for copy in load_t:
        copy.wait()
    send(blk(0, 0, 0), blk(0, 1, 0), ty_recv.at[0], YH)
    ring_up(0, 0)
    ring_down(0, 0)
    core_send(0, 0)

    for copy in load_m:
        copy.wait()

    def stage_moments(q, carry):
        for j in range(NDP):
            stage_m[j, q] = momf[q, :, j * 256 : (j + 1) * 256].astype(BF)
        return carry

    lax.fori_loop(0, 6, stage_moments, 0)

    def wb(p, dx, du, lo=0, n=512):
        return W.at[p, wrow(fs(dx, du), lo, n), :]

    def w_own(p):
        arrived(W.at[p, wrow(f, 0, 496), :], a_recv.at[p])
        send(wb(p, 0, 0), wb(p, 0, 0), w_recv.at[p, 2], YP)
        send(wb(p, 0, 0), wb(p, 0, 0), w_recv.at[p, 0], XP)
        send(wb(p, 0, 0), wb(p, 0, 0), w_recv.at[p, 1], XM)

    def w_partner(p):
        arrived(wb(p, 0, 1), w_recv.at[p, 2])
        if p < 2:
            send(wb(p, 0, 1), wb(p, 0, 1), w_recv.at[p, 3], XP)
            send(wb(p, 0, 1), wb(p, 0, 1), w_recv.at[p, 4], XM)

    def w_relay(p, du):
        arrived(wb(p, 3, du), w_recv.at[p, 3 * du])
        send(wb(p, 3, du, 0, 256), wb(p, 3, du, 0, 256), w_recv.at[p, 5 + 2 * du], XP)
        if p == 2:
            send(wb(p, 3, 0), wb(p, 3, 0), w_recv.at[p, 3], YP)
        arrived(wb(p, 1, du), w_recv.at[p, 3 * du + 1])
        send(wb(p, 1, du, 256, 256), wb(p, 1, du, 256, 256), w_recv.at[p, 6 + 2 * du], XM)
        if p == 2:
            send(wb(p, 1, 0), wb(p, 1, 0), w_recv.at[p, 4], YP)

    def w_far(p, du):
        arrived(wb(p, 2, du, 0, 256), w_recv.at[p, 5 + 2 * du])
        arrived(wb(p, 2, du, 256, 256), w_recv.at[p, 6 + 2 * du])

    w_own(0)
    arrived(blk(0, 1, 0), ty_recv.at[0])
    ring_up(0, 1)
    ring_down(0, 1)
    core_send(0, 1)
    w_own(1)
    w_partner(0)
    w_own(2)
    keep = pltpu.make_async_copy(W.at[:, wrow(f, 0, 512), :], mas_hbm, own_sems.at[0])
    keep.start()
    w_partner(1)
    ring_step(1, 0)
    w_relay(0, 0)
    w_relay(0, 1)
    ring_step(1, 1)
    w_relay(1, 0)
    w_partner(2)
    w_relay(2, 0)
    ring_step(2, 0)
    w_relay(1, 1)
    ring_step(2, 1)
    ring_step(3, 0)
    w_far(2, 0)
    send(wb(2, 2, 0), wb(2, 2, 0), w_recv.at[2, 7], YP)
    ring_step(3, 1)

    def give_moments(i, carry):
        to = other(i)
        pltpu.make_async_remote_copy(
            src_ref=stage_m.at[to],
            dst_ref=mom_hbm.at[:, mine16(0), :],
            send_sem=m_send.at[0],
            recv_sem=m_recv.at[0],
            device_id={"dp": to},
            device_id_type=MESH,
        ).start()
        return carry

    lax.fori_loop(1, NDP, give_moments, 0)
    keep_m = pltpu.make_async_copy(stage_m.at[d], mom_hbm.at[:, mine16(0), :], own_sems.at[1])
    keep_m.start()

    first_ones = NDP * n_old // (n_old + n_new)
    grown_at = jnp.maximum(d - first_ones, 0) * 256
    grown_scale = mask_ref[:, pl.ds(pl.multiple_of(grown_at, 256), 256)]
    is_grown = jnp.where(d >= first_ones, 1.0, 0.0)
    scale = is_grown * grown_scale + (1.0 - is_grown)

    def project(h, p):
        left = T[0 if p < 2 else 1, h * 256 : (h + 1) * 256, :]
        acc[p] = jnp.dot(left, W[p], preferred_element_type=F32)

    def pointwise(h):
        gate_value, up_value = acc[0], acc[1]
        sigmoid_gate = jax.nn.sigmoid(gate_value)
        activated = gate_value * sigmoid_gate
        hidden = activated * up_value * scale
        back_hidden = acc[2] * scale
        gate_back = (
            back_hidden * up_value * sigmoid_gate * (1.0 + gate_value * (1.0 - sigmoid_gate))
        )
        up_back = back_hidden * activated
        rounded = hidden.astype(BF)
        H[0, h * 128 : (h + 1) * 128] = rounded[:128]
        H[1, h * 128 : (h + 1) * 128] = rounded[128:]
        cols = slice(h * 256, (h + 1) * 256)
        XT[0:256, cols] = gate_back.T.astype(BF)
        XT[256:512, cols] = up_back.T.astype(BF)
        XT[512:768, cols] = hidden.T.astype(BF)

    for k in (0, 1, 7, 2):
        for u in (0, 1):
            arrived(blk(k, u, 1), tc_recv.at[k, u])
    w_far(0, 0)
    w_far(0, 1)
    project(0, 0)
    w_far(1, 0)
    w_far(1, 1)
    project(0, 1)
    for u in (0, 1):
        arrived(T.at[0, pl.ds(row(4, u, 0), 16), :], tz_recv.at[4, u])
        arrived(T.at[1, pl.ds(row(4, u, 0), 16), :], tz_recv.at[8, u])
        core_send(4, u)
    arrived(wb(2, 3, 1), w_recv.at[2, 3])
    arrived(wb(2, 1, 1), w_recv.at[2, 4])
    arrived(wb(2, 2, 1), w_recv.at[2, 7])
    project(0, 2)
    pointwise(0)
    for k in (6, 3, 5, 4):
        for u in (0, 1):
            arrived(blk(k, u, 1), tc_recv.at[k, u])
    project(1, 0)
    project(1, 1)
    project(1, 2)
    pointwise(1)

    def tcols(i, fi):
        return T[i, :, pl.ds(pl.multiple_of(fi * 512, 512), 512)]

    def grad_gu(dx, du):
        G[dx, du, 0:512] = jnp.dot(
            XT[0:512], tcols(0, fs(dx, du)), preferred_element_type=F32
        ).astype(BF)

    def grad_down(dx, du):
        G[dx, du, 512:768] = jnp.dot(
            XT[512:768], tcols(1, fs(dx, du)), preferred_element_type=F32
        ).astype(BF)

    def out_part(v):
        def chunk(j, carry):
            cols = pl.ds(pl.multiple_of(j * 512, 512), 512)
            O[v, :, cols] = lax.dot_general(
                H[v],
                W[2, cols, :],
                (((1,), (1,)), ((), ())),
                preferred_element_type=F32,
            ).astype(BF)
            return carry

        lax.fori_loop(0, 8, chunk, 0)

    def g_first(g, du, lo, n):
        a, b = pl.ds(lo, n // 2), pl.ds(lo + n // 2, n // 2)
        send(G.at[2, du, a, :], R1.at[du, a, :], r1_recv.at[g, 0], XP)
        send(G.at[2, du, b, :], R1.at[du, b, :], r1_recv.at[g, 1], XM)

    def g_second(g, du, lo, n):
        a, b = pl.ds(lo, n // 2), pl.ds(lo + n // 2, n // 2)
        arrived(R1.at[du, a, :], r1_recv.at[g, 0])
        G[1, du, a, :] = (G[1, du, a, :].astype(F32) + R1[du, a, :].astype(F32)).astype(BF)
        w = pl.ds(lo, n)
        send(G.at[1, du, w, :], R2m.at[du, w, :], r2m_recv.at[g], XP)
        arrived(R1.at[du, b, :], r1_recv.at[g, 1])
        G[3, du, b, :] = (G[3, du, b, :].astype(F32) + R1[du, b, :].astype(F32)).astype(BF)
        send(G.at[3, du, w, :], R2p.at[du, w, :], r2p_recv.at[g], XM)

    def g_third(g, du, lo, n):
        w = pl.ds(lo, n)
        arrived(R2m.at[du, w, :], r2m_recv.at[g])
        arrived(R2p.at[du, w, :], r2p_recv.at[g])
        return (
            G[0, du, w, :].astype(F32) + R2m[du, w, :].astype(F32) + R2p[du, w, :].astype(F32)
        )

    grad_gu(2, 1)
    g_first(1, 1, 0, 512)
    for dx in (2, 1, 3, 0):
        grad_down(dx, 1)
        send(G.at[dx, 1, pl.ds(512, 256), :], RYF.at[dx], ryf_recv.at[dx], YP)
    grad_gu(2, 0)
    g_first(0, 0, 0, 512)
    out_part(1)
    for h in (0, 1):
        rows = pl.ds(h * 128, 128)
        send(O.at[1, rows, :], RC.at[rows, :], rc_recv.at[h], CP)

    def down_sum(dx):
        arrived(RYF.at[dx], ryf_recv.at[dx])
        G[dx, 0, 512:768, :] = (
            jnp.dot(XT[512:768], tcols(1, fs(dx, 0)), preferred_element_type=F32)
            .astype(BF)
            .astype(F32)
            + RYF[dx].astype(F32)
        ).astype(BF)

    down_sum(2)
    g_first(2, 0, 512, 256)
    out_part(0)
    grad_gu(1, 1)
    grad_gu(3, 1)

    def zrows(k):
        return pl.ds(PLACE[k] * 32, 32)

    def core_sum(h):
        rows = pl.ds(h * 128, 128)
        arrived(RC.at[rows, :], rc_recv.at[h])
        PT[rows, :] = (O[0, rows, :].astype(F32) + RC[rows, :].astype(F32)).astype(BF)

    core_sum(1)
    left, right = pl.ds(0, 2048), pl.ds(2048, 2048)
    send(PT.at[zrows(4), left], RZp.at[0, :, left], rzp_recv.at[0], ZP)
    send(PT.at[zrows(4), right], RZm.at[0, :, right], rzm_recv.at[0], ZM)
    core_sum(0)

    def z_step(s):
        whole = pl.ds(0, 4096)
        for k, got, sem, cols, to in (
            (4 - s, RZp, rzp_recv, left if s == 1 else whole, ZP),
            (4 + s, RZm, rzm_recv, right if s == 1 else whole, ZM),
        ):
            arrived(got.at[s - 1, :, cols], sem.at[s - 1])
            PT[zrows(k), cols] = (
                PT[zrows(k), cols].astype(F32) + got[s - 1, :, cols].astype(F32)
            ).astype(BF)
            send(PT.at[zrows(k), :], got.at[s], sem.at[s], to)

    g_second(1, 1, 0, 512)
    z_step(1)
    grad_gu(1, 0)
    grad_gu(3, 0)
    g_second(0, 0, 0, 512)
    z_step(2)
    down_sum(1)
    down_sum(3)
    g_second(2, 0, 512, 256)
    grad_gu(0, 1)
    grad_gu(0, 0)
    down_sum(0)
    z_step(3)

    G[0, 1, 0:512] = g_third(1, 1, 0, 512).astype(BF)
    send(G.at[0, 1, pl.ds(0, 512), :], RY, ry_recv.at[0], YP)

    arrived(RZp.at[3], rzp_recv.at[3])
    arrived(RZm.at[3], rzm_recv.at[3])
    near = PT[zrows(0), :].astype(F32) + RZp[3].astype(F32) + RZm[3].astype(F32)
    PT[16:32, :] = near[16:].astype(BF)
    send(PT.at[pl.ds(16, 16), :], RYH, ryh_recv.at[0], YH)

    grad_ref[2] = g_third(2, 0, 512, 256).T
    both = g_third(0, 0, 0, 512)
    arrived(RYH, ryh_recv.at[0])
    out_ref[...] = (near[:16] + RYH[...].astype(F32)).astype(BF)
    arrived(RY, ry_recv.at[0])
    both = both + RY[...].astype(F32)
    grad_ref[0] = both[:256].T
    grad_ref[1] = both[256:].T

    arrived(mom_hbm.at[:, pl.ds(0, 496), :], m_recv.at[0])
    for p in range(3):
        pltpu.make_async_copy(
            stage_w.at[p, pl.ds(0, 31)], stage_w.at[p, pl.ds(0, 31)], a_send.at[p]
        ).wait()
    pltpu.make_async_copy(
        stage_m.at[pl.ds(0, 31)], stage_m.at[pl.ds(0, 31)], m_send.at[0]
    ).wait()
    keep.wait()
    keep_m.wait()
    for copy in sent:
        copy.wait_send()


def local(
    tokens,
    upstream,
    old_master,
    old_first,
    old_second,
    grown_master,
    grown_first,
    grown_second,
    grow_mask,
):
    planes = tuple(
        jnp.transpose(a, (1, 0, 2))
        for a in (old_master, old_first, old_second, grown_master, grown_first, grown_second)
    )
    anyspace = pl.BlockSpec(memory_space=pl.ANY)
    vmem = pl.BlockSpec(memory_space=pltpu.VMEM)
    dma = pltpu.SemaphoreType.DMA
    out, gradients, moments, master = pl.pallas_call(
        step_kernel,
        out_shape=(
            jax.ShapeDtypeStruct((16, 4096), BF),
            jax.ShapeDtypeStruct((3, 512, 256), F32),
            jax.ShapeDtypeStruct((6, 512, 256), BF),
            jax.ShapeDtypeStruct((3, 512, 256), BF),
        ),
        in_specs=[anyspace] * 8 + [vmem],
        out_specs=(vmem, vmem, anyspace, anyspace),
        scratch_shapes=[
            pltpu.VMEM((3, 16, 8192), F32),
            pltpu.VMEM((6, 16, 8192), F32),
            pltpu.VMEM((3, 32, 16, 256), BF),
            pltpu.VMEM((32, 6, 16, 256), BF),
            pltpu.VMEM((3, 4096, 256), BF),
            pltpu.VMEM((2, 512, 4096), BF),
            pltpu.VMEM((3, 256, 256), F32),
            pltpu.VMEM((2, 256, 256), BF),
            pltpu.VMEM((768, 512), BF),
            pltpu.VMEM((4, 2, 768, 512), BF),
            pltpu.VMEM((2, 768, 512), BF),
            pltpu.VMEM((2, 768, 512), BF),
            pltpu.VMEM((2, 768, 512), BF),
            pltpu.VMEM((512, 512), BF),
            pltpu.VMEM((4, 256, 512), BF),
            pltpu.VMEM((2, 256, 4096), BF),
            pltpu.VMEM((256, 4096), BF),
            pltpu.VMEM((256, 4096), BF),
            pltpu.VMEM((4, 32, 4096), BF),
            pltpu.VMEM((4, 32, 4096), BF),
            pltpu.VMEM((16, 4096), BF),
            dma((12,)),
            dma((96,)),
            dma((3,)),
            dma((3,)),
            dma((1,)),
            dma((1,)),
            dma((2,)),
            dma((9, 2)),
            dma((8, 2)),
            dma((1,)),
            dma((3, 9)),
            dma((3, 2)),
            dma((3,)),
            dma((3,)),
            dma((1,)),
            dma((4,)),
            dma((2,)),
            dma((4,)),
            dma((4,)),
            dma((1,)),
        ],
        compiler_params=pltpu.CompilerParams(
            collective_id=0, has_side_effects=True, vmem_limit_bytes=64000 * 1024
        ),
        name="grown_step",
    )(tokens, upstream, *planes, grow_mask.reshape(1, -1))
    moments = moments.astype(F32)
    updated = adam_update(master.astype(F32), moments[:3], moments[3:], gradients)
    return (out,) + tuple(jnp.transpose(a, (1, 0, 2)) for a in updated)


def solution(mesh):
    rows = P(("fsdp", "dp"), None)
    stored = P(("fsdp", "dp"), None, None)
    owned = P("fsdp", None, "dp")
    return jax.shard_map(
        local,
        mesh=mesh,
        in_specs=(rows, rows) + (stored,) * 6 + (P(),),
        out_specs=(rows, owned, owned, owned),
        check_vma=False,
    )
```

time: 520 us -> 146 us (0.28)
  the two profiles are of different devices: /device:TPU:1 before, /device:TPU:14 now
where the time goes in v1:
time: 146 us
  Pallas kernels  139 us (95%)
  other arithmetic  4.83 us (3%)
  local copies, waits for them, and re-layouts  2.19 us (2%)
    pallas_call x1, Pallas kernels, local(): pl.pallas_call(step_kernel, out_shape=(jax.ShapeDtypeStruct((16, 4096), B...  139 us
    transpose x1, other arithmetic, local(): return (out,) + tuple((jnp.transpose(a, (1, 0, 2)) for a in updated))  2.99 us

profile of v1, /device:TPU:14, one launch (start us, length us, event | category | flops | bytes accessed | tf_op | source)
XLA Modules:
  0.0 146.3 jit_solution(14006419495700953838)
XLA Ops:
  0.6 1.3 reshape.11.mask_ref
  1.9 138.6 %grown_step.1 = (bf16[16,4096]{1,0:T(8,128)(2,1)}, f32[3,512,256]{2,1,0:T(8,128)}, bf16[6,512,256]{2,1,0:T(8,128)(2,1)}, bf16[3,512,256]{2,1,0:T(8,128)(2,1)}) custom-call(bf16[16,4096]{1,0:T(8,128)(2,1)} %tok_hbm.1, bf16[16,4096]{1,0:T(8,128)(2,1)} %ups_hbm.1, f32[3,16,5632]{2,1,0:T(8,128)} %bitcast.12, f32[3,16,5632]{2,1,0:T(8,128)} %bitcast.13, ...), custom_call_target="tpu_custom_call" | custom-call | tf_op jit(solution)/shard_map/grown_step/pallas_call | solution.py:554
  140.5 0.0 copy-start
  140.5 0.0 copy-start.1
  140.5 1.8 %convert_element_type.7 = f32[6,512,256]{2,1,0:T(8,128)S(1)} convert(bf16[6,512,256]{2,1,0:T(8,128)(2,1)} %get-tuple-element.10) | non-fusion elementwise | flops 786432 | bytes 4718592 | tf_op jit(solution)/shard_map/convert_element_type | solution.py:612
  142.4 0.0 copy-done
  142.4 0.2 copy-done.1
  142.6 0.0 copy-start.2
  142.6 3.0 %fusion.6 = (f32[512,3,256]{2,0,1:T(8,128)}, f32[512,3,256]{2,0,1:T(8,128)}, f32[512,3,256]{2,0,1:T(8,128)}) fusion(f32[3,512,256]{2,1,0:T(8,128)S(1)} %copy-done, f32[6,512,256]{2,1,0:T(8,128)S(1)} %convert_element_type.7, bf16[3,512,256]{2,1,0:T(8,128)(2,1)S(1)} %copy-done.1), kind=kLoop, calls=%fused_computation.11 | loop fusion | flops 5898240 | bytes 10223616 | tf_op jit(solution)/shard_map/transpose | solution.py:614
  145.6 0.0 copy-done.2
  145.6 0.7 copy.14
Async XLA Ops:
  140.5 1.9 %copy-start = (f32[3,512,256]{2,1,0:T(8,128)S(1)}, f32[3,512,256]{2,1,0:T(8,128)}, u32[]{:S(2)}) copy-start(f32[3,512,256]{2,1,0:T(8,128)} %get-tuple-element.11) | copy-start | bytes 4718596
  140.5 2.1 %copy-start.1 = (bf16[3,512,256]{2,1,0:T(8,128)(2,1)S(1)}, bf16[3,512,256]{2,1,0:T(8,128)(2,1)}, u32[]{:S(2)}) copy-start(bf16[3,512,256]{2,1,0:T(8,128)(2,1)} %get-tuple-element.9) | copy-start | bytes 2359300
  142.6 3.0 %copy-start.2 = (bf16[16,4096]{1,0:T(8,128)(2,1)S(1)}, bf16[16,4096]{1,0:T(8,128)(2,1)}, u32[]{:S(2)}) copy-start(bf16[16,4096]{1,0:T(8,128)(2,1)} %get-tuple-element.19) | copy-start | bytes 393220

commit v2 on v1

--- a/solution.py
+++ b/solution.py
@@ -20,6 +20,7 @@
 MESH = pl.DeviceIdType.MESH
 
 NX, NZ, NDP = 4, 8, 32
+MOMENTS = (16, 22, 25, 28, 30, 32, 32)
 PLACE = {k: i for i, k in enumerate((0, 1, 7, 2, 6, 3, 5, 4))}
 
 
@@ -46,7 +47,8 @@
     mask_ref,
     out_ref,
     grad_ref,
-    mom_hbm,
+    fst_hbm,
+    snd_hbm,
     mas_hbm,
     mf,
     momf,
@@ -106,7 +108,8 @@
 
     XP, XM, YP = {"fsdp": fs(1, 0)}, {"fsdp": fs(3, 0)}, {"fsdp": fs(0, 1)}
     ZP, ZM = {"dp": dpi(1, 0, 0)}, {"dp": dpi(7, 0, 0)}
-    YH, CP = {"dp": dpi(0, 1, 0)}, {"dp": dpi(0, 0, 1)}
+    CP = {"dp": dpi(0, 0, 1)}
+    YN = {"dp": dpi(0, 1, 0), "fsdp": fs(0, 1)}
 
     sent = []
 
@@ -175,7 +178,7 @@
         return carry
 
     lax.fori_loop(1, NDP, greet, 0)
-    for dev in (XP, XM, YP):
+    for dev in (XP, XM, YP, YN):
         pl.semaphore_signal(barrier, inc=1, device_id=dev, device_id_type=MESH)
 
     def wrow(fi, lo, n):
@@ -191,7 +194,7 @@
             stage_w[p, j] = mf[p, :, j * 256 : (j + 1) * 256].astype(BF)
         W[p, mine16(f * 512), :] = stage_w[p, d]
         if p == 0:
-            pl.semaphore_wait(barrier, NDP - 1 + 3)
+            pl.semaphore_wait(barrier, NDP - 1 + 4)
 
         def give(i, carry, p=p):
             to = other(i)
@@ -207,48 +210,60 @@
 
         lax.fori_loop(1, NDP, give, 0)
 
-    def core_send(k, u):
-        send(blk(k, u, 0), blk(k, u, 1), tc_recv.at[k, u], CP)
-
-    def ring_up(s, u):
-        a, b = (8 - s) % 8, 7 - s
-        if b == 4:
-            send(
-                T.at[0, pl.ds(row(a, u, 0), 16), :],
-                T.at[0, pl.ds(row(b, u, 0), 16), :],
-                tz_recv.at[4, u],
-                ZP,
-            )
-        else:
-            send(blk(a, u, 0), blk(b, u, 0), tz_recv.at[b, u], ZP)
-
-    def ring_down(s, u):
-        a, b = s, s + 1
-        if b == 4:
-            send(
-                T.at[1, pl.ds(row(a, u, 0), 16), :],
-                T.at[1, pl.ds(row(b, u, 0), 16), :],
-                tz_recv.at[8, u],
-                ZM,
-            )
-        else:
-            send(blk(a, u, 0), blk(b, u, 0), tz_recv.at[b, u], ZM)
-
-    def ring_step(s, u):
-        up, down = (8 - s) % 8, s
-        arrived(blk(up, u, 0), tz_recv.at[up, u])
-        ring_up(s, u)
-        arrived(blk(down, u, 0), tz_recv.at[down, u])
-        ring_down(s, u)
-        core_send(up, u)
-        core_send(down, u)
+    def piece(i, k, u, v=0):
+        return T.at[i, pl.ds(row(k, u, v), 16), :]
+
+    def core_send(i, k, u):
+        send(piece(i, k, u), piece(i, k, u, 1), tc_recv.at[k, u, i], CP)
+
+    def side_send(i, k):
+        send(piece(i, k, 0), piece(i, k, 1), ty_recv.at[k, i], YN)
+
+    left, right = pl.ds(0, 2048), pl.ds(2048, 2048)
+    streams = ((0, 0), (1, 0), (0, 1))
+
+    def ring_piece(j, k, down):
+        i, u = streams[j]
+        if k != 4:
+            return piece(i, k, u), tz_recv.at[k, j]
+        if j == 2:
+            half = right if down else left
+            return T.at[i, pl.ds(row(k, u, 0), 16), half], tz_recv.at[0 if down else 4, j]
+        return (piece(i, k, u), tz_recv.at[4, j]) if j == down else (None, None)
+
+    def ring_send(j, s, down):
+        a, b = (s, s + 1) if down else ((8 - s) % 8, 7 - s)
+        dst, sem = ring_piece(j, b, down)
+        if dst is None:
+            return
+        i, u = streams[j]
+        src = piece(i, a, u)
+        if b == 4 and j == 2:
+            src = T.at[i, pl.ds(row(a, u, 0), 16), right if down else left]
+        send(src, dst, sem, ZM if down else ZP)
+
+    def ring_step(s):
+        for j, (i, u) in enumerate(streams):
+            for down in (0, 1):
+                k = s if down else (8 - s) % 8
+                arrived(piece(i, k, u), tz_recv.at[k, j])
+                ring_send(j, s, down)
+            for k in ((8 - s) % 8, s):
+                if j == 1:
+                    side_send(1, k)
+                core_send(i, k, u)
+
+    def side_arrived(k):
+        arrived(piece(1, k, 1), ty_recv.at[k, 1])
+        core_send(1, k, 1)
 
     for copy in load_t:
         copy.wait()
-    send(blk(0, 0, 0), blk(0, 1, 0), ty_recv.at[0], YH)
-    ring_up(0, 0)
-    ring_down(0, 0)
-    core_send(0, 0)
+    for i in (0, 1):
+        side_send(i, 0)
+        for down in (0, 1):
+            ring_send(i, 0, down)
+        core_send(i, 0, 0)
 
     for copy in load_m:
         copy.wait()
@@ -290,46 +305,73 @@
         arrived(wb(p, 2, du, 256, 256), w_recv.at[p, 6 + 2 * du])
 
     w_own(0)
-    arrived(blk(0, 1, 0), ty_recv.at[0])
-    ring_up(0, 1)
-    ring_down(0, 1)
-    core_send(0, 1)
+    arrived(piece(0, 0, 1), ty_recv.at[0, 0])
+    for down in (0, 1):
+        ring_send(2, 0, down)
+    core_send(0, 0, 1)
+    side_arrived(0)
     w_own(1)
     w_partner(0)
     w_own(2)
     keep = pltpu.make_async_copy(W.at[:, wrow(f, 0, 512), :], mas_hbm, own_sems.at[0])
     keep.start()
+    ring_step(1)
     w_partner(1)
-    ring_step(1, 0)
     w_relay(0, 0)
+    ring_step(2)
+    w_relay(2, 0)
     w_relay(0, 1)
-    ring_step(1, 1)
     w_relay(1, 0)
+    ring_step(3)
+    w_relay(1, 1)
     w_partner(2)
-    w_relay(2, 0)
-    ring_step(2, 0)
-    w_relay(1, 1)
-    ring_step(2, 1)
-    ring_step(3, 0)
-    w_far(2, 0)
-    send(wb(2, 2, 0), wb(2, 2, 0), w_recv.at[2, 7], YP)
-    ring_step(3, 1)
 
     def give_moments(i, carry):
-        to = other(i)
-        pltpu.make_async_remote_copy(
-            src_ref=stage_m.at[to],
-            dst_ref=mom_hbm.at[:, mine16(0), :],
-            send_sem=m_send.at[0],
-            recv_sem=m_recv.at[0],
-            device_id={"dp": to},
-            device_id_type=MESH,
-        ).start()
+        r = lax.rem(i, 16)
+        turn = (1 - 2 * lax.rem(r + 1, 2)) * lax.div(r + 1, 2)
+        there = yh + lax.div(i, 16) * (1 - 2 * yh)
+        to = there * 16 + lax.rem(lax.rem(d, 16) + 16 + turn, 16)
+        for half, dst in enumerate((fst_hbm, snd_hbm)):
+            pltpu.make_async_remote_copy(
+                src_ref=stage_m.at[to, pl.ds(3 * half, 3)],
+                dst_ref=dst.at[:, mine16(0), :],
+                send_sem=m_send.at[half],
+                recv_sem=m_recv.at[half],
+                device_id={"dp": to},
+                device_id_type=MESH,
+            ).start()
         return carry
 
-    lax.fori_loop(1, NDP, give_moments, 0)
-    keep_m = pltpu.make_async_copy(stage_m.at[d], mom_hbm.at[:, mine16(0), :], own_sems.at[1])
-    keep_m.start()
+    given = [1]
+
+    def moments_to(n):
+        lax.fori_loop(given[0], n, give_moments, 0)
+        given[0] = n
+
+    keep_m = [
+        pltpu.make_async_copy(
+            stage_m.at[d, pl.ds(3 * half, 3)], dst.at[:, mine16(0), :], own_sems.at[1 + half]
+        )
+        for half, dst in enumerate((fst_hbm, snd_hbm))
+    ]
+    for copy in keep_m:
+        copy.start()
+    moments_to(MOMENTS[0])
+
+    side_arrived(7)
+    side_arrived(1)
+    side_arrived(6)
+    side_arrived(2)
+    arrived(piece(0, 4, 0), tz_recv.at[4, 0])
+    core_send(0, 4, 0)
+    arrived(piece(1, 4, 0), tz_recv.at[4, 1])
+    side_send(1, 4)
+    core_send(1, 4, 0)
+    side_arrived(5)
+    side_arrived(3)
+    for down in (0, 1):
+        arrived(*ring_piece(2, 4, down))
+    core_send(0, 4, 1)
 
     first_ones = NDP * n_old // (n_old + n_new)
     grown_at = jnp.maximum(d - first_ones, 0) * 256
@@ -337,16 +379,28 @@
     is_grown = jnp.where(d >= first_ones, 1.0, 0.0)
     scale = is_grown * grown_scale + (1.0 - is_grown)
 
-    def project(h, p):
-        left = T[0 if p < 2 else 1, h * 256 : (h + 1) * 256, :]
-        acc[p] = jnp.dot(left, W[p], preferred_element_type=F32)
+    near, far = ((0, 0), (0, 1), (1, 0), (3, 0), (1, 1), (3, 1)), ((2, 0), (2, 1))
+
+    def project(p, blocks, start):
+        for h in (0, 1):
+            total = None if start else acc[h, p]
+            for dx, du in blocks:
+                fi = fs(dx, du)
+                at = pl.ds(pl.multiple_of(fi * 512, 512), 512)
+                part = jnp.dot(
+                    T[0 if p < 2 else 1, h * 256 : (h + 1) * 256, at],
+                    W[p, at, :],
+                    preferred_element_type=F32,
+                )
+                total = part if total is None else total + part
+            acc[h, p] = total
 
     def pointwise(h):
-        gate_value, up_value = acc[0], acc[1]
+        gate_value, up_value = acc[h, 0], acc[h, 1]
         sigmoid_gate = jax.nn.sigmoid(gate_value)
         activated = gate_value * sigmoid_gate
         hidden = activated * up_value * scale
-        back_hidden = acc[2] * scale
+        back_hidden = acc[h, 2] * scale
         gate_back = (
             back_hidden * up_value * sigmoid_gate * (1.0 + gate_value * (1.0 - sigmoid_gate))
         )
@@ -359,30 +413,30 @@
         XT[256:512, cols] = up_back.T.astype(BF)
         XT[512:768, cols] = hidden.T.astype(BF)
 
-    for k in (0, 1, 7, 2):
-        for u in (0, 1):
-            arrived(blk(k, u, 1), tc_recv.at[k, u])
+    for i in (0, 1):
+        for k in (0, 1, 7, 2, 6, 3, 5, 4):
+            for u in (0, 1):
+                if (i, k, u) != (1, 4, 1):
+                    arrived(piece(i, k, u, 1), tc_recv.at[k, u, i])
+    project(0, near, True)
+    w_far(2, 0)
+    send(wb(2, 2, 0), wb(2, 2, 0), w_recv.at[2, 7], YP)
+    moments_to(MOMENTS[1])
+    project(1, near, True)
     w_far(0, 0)
     w_far(0, 1)
-    project(0, 0)
+    project(0, far, False)
+    arrived(wb(2, 3, 1), w_recv.at[2, 3])
+    arrived(wb(2, 1, 1), w_recv.at[2, 4])
+    side_arrived(4)
+    arrived(piece(1, 4, 1, 1), tc_recv.at[4, 1, 1])
+    project(2, near, True)
     w_far(1, 0)
     w_far(1, 1)
-    project(0, 1)
-    for u in (0, 1):
-        arrived(T.at[0, pl.ds(row(4, u, 0), 16), :], tz_recv.at[4, u])
-        arrived(T.at[1, pl.ds(row(4, u, 0), 16), :], tz_recv.at[8, u])
-        core_send(4, u)
-    arrived(wb(2, 3, 1), w_recv.at[2, 3])
-    arrived(wb(2, 1, 1), w_recv.at[2, 4])
+    project(1, far, False)
     arrived(wb(2, 2, 1), w_recv.at[2, 7])
-    project(0, 2)
+    project(2, far, False)
     pointwise(0)
-    for k in (6, 3, 5, 4):
-        for u in (0, 1):
-            arrived(blk(k, u, 1), tc_recv.at[k, u])
-    project(1, 0)
-    project(1, 1)
-    project(1, 2)
     pointwise(1)
 
     def tcols(i, fi):
@@ -436,15 +490,16 @@
 
     grad_gu(2, 1)
     g_first(1, 1, 0, 512)
-    for dx in (2, 1, 3, 0):
-        grad_down(dx, 1)
-        send(G.at[dx, 1, pl.ds(512, 256), :], RYF.at[dx], ryf_recv.at[dx], YP)
     grad_gu(2, 0)
     g_first(0, 0, 0, 512)
     out_part(1)
     for h in (0, 1):
         rows = pl.ds(h * 128, 128)
         send(O.at[1, rows, :], RC.at[rows, :], rc_recv.at[h], CP)
+    for dx in (2, 1, 3, 0):
+        grad_down(dx, 1)
+        send(G.at[dx, 1, pl.ds(512, 256), :], RYF.at[dx], ryf_recv.at[dx], YP)
+    out_part(0)
 
     def down_sum(dx):
         arrived(RYF.at[dx], ryf_recv.at[dx])
@@ -455,12 +510,6 @@
             + RYF[dx].astype(F32)
         ).astype(BF)
 
-    down_sum(2)
-    g_first(2, 0, 512, 256)
-    out_part(0)
-    grad_gu(1, 1)
-    grad_gu(3, 1)
-
     def zrows(k):
         return pl.ds(PLACE[k] * 32, 32)
 
@@ -470,10 +519,14 @@
         PT[rows, :] = (O[0, rows, :].astype(F32) + RC[rows, :].astype(F32)).astype(BF)
 
     core_sum(1)
-    left, right = pl.ds(0, 2048), pl.ds(2048, 2048)
     send(PT.at[zrows(4), left], RZp.at[0, :, left], rzp_recv.at[0], ZP)
     send(PT.at[zrows(4), right], RZm.at[0, :, right], rzm_recv.at[0], ZM)
+    moments_to(MOMENTS[2])
     core_sum(0)
+    down_sum(2)
+    g_first(2, 0, 512, 256)
+    grad_gu(1, 1)
+    grad_gu(3, 1)
 
     def z_step(s):
         whole = pl.ds(0, 4096)
@@ -489,10 +542,12 @@
 
     g_second(1, 1, 0, 512)
     z_step(1)
+    moments_to(MOMENTS[3])
     grad_gu(1, 0)
     grad_gu(3, 0)
     g_second(0, 0, 0, 512)
     z_step(2)
+    moments_to(MOMENTS[4])
     down_sum(1)
     down_sum(3)
     g_second(2, 0, 512, 256)
@@ -500,35 +555,39 @@
     grad_gu(0, 0)
     down_sum(0)
     z_step(3)
+    moments_to(MOMENTS[5])
 
     G[0, 1, 0:512] = g_third(1, 1, 0, 512).astype(BF)
     send(G.at[0, 1, pl.ds(0, 512), :], RY, ry_recv.at[0], YP)
 
     arrived(RZp.at[3], rzp_recv.at[3])
     arrived(RZm.at[3], rzm_recv.at[3])
-    near = PT[zrows(0), :].astype(F32) + RZp[3].astype(F32) + RZm[3].astype(F32)
-    PT[16:32, :] = near[16:].astype(BF)
-    send(PT.at[pl.ds(16, 16), :], RYH, ryh_recv.at[0], YH)
+    nearby = PT[zrows(0), :].astype(F32) + RZp[3].astype(F32) + RZm[3].astype(F32)
+    PT[16:32, :] = nearby[16:].astype(BF)
+    send(PT.at[pl.ds(16, 16), :], RYH, ryh_recv.at[0], YN)
+    moments_to(MOMENTS[6])
 
     grad_ref[2] = g_third(2, 0, 512, 256).T
     both = g_third(0, 0, 0, 512)
     arrived(RYH, ryh_recv.at[0])
-    out_ref[...] = (near[:16] + RYH[...].astype(F32)).astype(BF)
+    out_ref[...] = (nearby[:16] + RYH[...].astype(F32)).astype(BF)
     arrived(RY, ry_recv.at[0])
     both = both + RY[...].astype(F32)
     grad_ref[0] = both[:256].T
     grad_ref[1] = both[256:].T
 
-    arrived(mom_hbm.at[:, pl.ds(0, 496), :], m_recv.at[0])
+    for half, dst in enumerate((fst_hbm, snd_hbm)):
+        arrived(dst.at[:, pl.ds(0, 496), :], m_recv.at[half])
     for p in range(3):
         pltpu.make_async_copy(
             stage_w.at[p, pl.ds(0, 31)], stage_w.at[p, pl.ds(0, 31)], a_send.at[p]
         ).wait()
-    pltpu.make_async_copy(
-        stage_m.at[pl.ds(0, 31)], stage_m.at[pl.ds(0, 31)], m_send.at[0]
-    ).wait()
+    for half in (0, 1):
+        given_all = stage_m.at[pl.ds(0, 31), pl.ds(3 * half, 3)]
+        pltpu.make_async_copy(given_all, given_all, m_send.at[half]).wait()
     keep.wait()
-    keep_m.wait()
+    for copy in keep_m:
+        copy.wait()
     for copy in sent:
         copy.wait_send()
 
@@ -551,16 +610,17 @@
     anyspace = pl.BlockSpec(memory_space=pl.ANY)
     vmem = pl.BlockSpec(memory_space=pltpu.VMEM)
     dma = pltpu.SemaphoreType.DMA
-    out, gradients, moments, master = pl.pallas_call(
+    out, gradients, first, second, master = pl.pallas_call(
         step_kernel,
         out_shape=(
             jax.ShapeDtypeStruct((16, 4096), BF),
             jax.ShapeDtypeStruct((3, 512, 256), F32),
-            jax.ShapeDtypeStruct((6, 512, 256), BF),
+            jax.ShapeDtypeStruct((3, 512, 256), BF),
+            jax.ShapeDtypeStruct((3, 512, 256), BF),
             jax.ShapeDtypeStruct((3, 512, 256), BF),
         ),
         in_specs=[anyspace] * 8 + [vmem],
-        out_specs=(vmem, vmem, anyspace, anyspace),
+        out_specs=(vmem, vmem, anyspace, anyspace, anyspace),
         scratch_shapes=[
             pltpu.VMEM((3, 16, 8192), F32),
             pltpu.VMEM((6, 16, 8192), F32),
@@ -568,7 +628,7 @@
             pltpu.VMEM((32, 6, 16, 256), BF),
             pltpu.VMEM((3, 4096, 256), BF),
             pltpu.VMEM((2, 512, 4096), BF),
-            pltpu.VMEM((3, 256, 256), F32),
+            pltpu.VMEM((2, 3, 256, 256), F32),
             pltpu.VMEM((2, 256, 256), BF),
             pltpu.VMEM((768, 512), BF),
             pltpu.VMEM((4, 2, 768, 512), BF),
@@ -584,15 +644,15 @@
             pltpu.VMEM((4, 32, 4096), BF),
             pltpu.VMEM((16, 4096), BF),
             dma((12,)),
-            dma((96,)),
+            dma((160,)),
             dma((3,)),
             dma((3,)),
-            dma((1,)),
-            dma((1,)),
             dma((2,)),
-            dma((9, 2)),
+            dma((2,)),
+            dma((3,)),
+            dma((8, 3)),
+            dma((8, 2, 2)),
             dma((8, 2)),
-            dma((1,)),
             dma((3, 9)),
             dma((3, 2)),
             dma((3,)),
@@ -609,8 +669,9 @@
         ),
         name="grown_step",
     )(tokens, upstream, *planes, grow_mask.reshape(1, -1))
-    moments = moments.astype(F32)
-    updated = adam_update(master.astype(F32), moments[:3], moments[3:], gradients)
+    updated = adam_update(
+        master.astype(F32), first.astype(F32), second.astype(F32), gradients
+    )
     return (out,) + tuple(jnp.transpose(a, (1, 0, 2)) for a in updated)
 
 

time: 146 us -> 139 us (0.952)
  the two profiles are of different devices: /device:TPU:14 before, /device:TPU:1 now
where the time goes in v2:
time: 139 us
  Pallas kernels  131 us (94%)
  other arithmetic  5.55 us (4%)
  local copies, waits for them, and re-layouts  1.97 us (1%)
    pallas_call x1, Pallas kernels, local(): pl.pallas_call(step_kernel, out_shape=(jax.ShapeDtypeStruct((16, 4096), B...  131 us
    transpose x1, other arithmetic, local(): return (out,) + tuple((jnp.transpose(a, (1, 0, 2)) for a in updated))  5.55 us

profile of v2, /device:TPU:1, one launch (start us, length us, event | category | flops | bytes accessed | tf_op | source)
XLA Modules:
  0.0 139.0 jit_solution(17121889888014546057)
XLA Ops:
  0.6 1.3 reshape.11.mask_ref
  1.9 130.8 %grown_step.1 = (bf16[16,4096]{1,0:T(8,128)(2,1)}, f32[3,512,256]{2,1,0:T(8,128)}, bf16[3,512,256]{2,1,0:T(8,128)(2,1)}, bf16[3,512,256]{2,1,0:T(8,128)(2,1)}, bf16[3,512,256]{2,1,0:T(8,128)(2,1)}) custom-call(bf16[16,4096]{1,0:T(8,128)(2,1)} %tok_hbm.1, bf16[16,4096]{1,0:T(8,128)(2,1)} %ups_hbm.1, f32[3,16,5632]{2,1,0:T(8,128)} %bitcast.12, ...), custom_call_target="tpu_custom_call" | custom-call | tf_op jit(solution)/shard_map/grown_step/pallas_call | solution.py:613
  132.8 0.0 copy-start
  132.8 5.6 %fusion.5 = (f32[512,3,256]{2,0,1:T(8,128)}, f32[512,3,256]{2,0,1:T(8,128)}, f32[512,3,256]{2,0,1:T(8,128)}) fusion(f32[3,512,256]{2,1,0:T(8,128)} %get-tuple-element.12, bf16[3,512,256]{2,1,0:T(8,128)(2,1)} %get-tuple-element.13, bf16[3,512,256]{2,1,0:T(8,128)(2,1)} %get-tuple-element.11, bf16[3,512,256]{2,1,0:T(8,128)(2,1)} %get-tuple-element.10), kind=kLoop, calls=%fused_computation.9 | loop fusion | flops 6684672 | bytes 8650752 | tf_op jit(solution)/shard_map/transpose | solution.py:675
  138.4 0.0 copy-done
  138.4 0.7 copy.14
Async XLA Ops:
  132.8 5.6 %copy-start = (bf16[16,4096]{1,0:T(8,128)(2,1)S(1)}, bf16[16,4096]{1,0:T(8,128)(2,1)}, u32[]{:S(2)}) copy-start(bf16[16,4096]{1,0:T(8,128)(2,1)} %get-tuple-element.21) | copy-start | bytes 393220

commit v3 on v2

--- a/solution.py
+++ b/solution.py
@@ -20,7 +20,9 @@
 MESH = pl.DeviceIdType.MESH
 
 NX, NZ, NDP = 4, 8, 32
-MOMENTS = (16, 22, 25, 28, 30, 32, 32)
+MOMENTS = (
+    (0, 0), (0, 0), (0, 0), (0, 0), (15, 0), (15, 4), (15, 7), (15, 10), (15, 13), (15, 16), (15, 16),
+)
 PLACE = {k: i for i, k in enumerate((0, 1, 7, 2, 6, 3, 5, 4))}
 
 
@@ -64,6 +66,7 @@
     R2m,
     R2p,
     RY,
+    RYS,
     RYF,
     O,
     RC,
@@ -304,28 +307,6 @@
         arrived(wb(p, 2, du, 0, 256), w_recv.at[p, 5 + 2 * du])
         arrived(wb(p, 2, du, 256, 256), w_recv.at[p, 6 + 2 * du])
 
-    w_own(0)
-    arrived(piece(0, 0, 1), ty_recv.at[0, 0])
-    for down in (0, 1):
-        ring_send(2, 0, down)
-    core_send(0, 0, 1)
-    side_arrived(0)
-    w_own(1)
-    w_partner(0)
-    w_own(2)
-    keep = pltpu.make_async_copy(W.at[:, wrow(f, 0, 512), :], mas_hbm, own_sems.at[0])
-    keep.start()
-    ring_step(1)
-    w_partner(1)
-    w_relay(0, 0)
-    ring_step(2)
-    w_relay(2, 0)
-    w_relay(0, 1)
-    w_relay(1, 0)
-    ring_step(3)
-    w_relay(1, 1)
-    w_partner(2)
-
     def give_moments(i, carry):
         r = lax.rem(i, 16)
         turn = (1 - 2 * lax.rem(r + 1, 2)) * lax.div(r + 1, 2)
@@ -342,11 +323,14 @@
             ).start()
         return carry
 
-    given = [1]
-
-    def moments_to(n):
-        lax.fori_loop(given[0], n, give_moments, 0)
-        given[0] = n
+    given = [1, 16]
+
+    def moments_to(point):
+        for side, n in enumerate(MOMENTS[point]):
+            n += 1 + 15 * side
+            if n > given[side]:
+                lax.fori_loop(given[side], n, give_moments, 0)
+                given[side] = n
 
     keep_m = [
         pltpu.make_async_copy(
@@ -356,7 +340,34 @@
     ]
     for copy in keep_m:
         copy.start()
-    moments_to(MOMENTS[0])
+
+    w_own(0)
+    moments_to(0)
+    arrived(piece(0, 0, 1), ty_recv.at[0, 0])
+    for down in (0, 1):
+        ring_send(2, 0, down)
+    core_send(0, 0, 1)
+    side_arrived(0)
+    w_own(1)
+    w_partner(0)
+    w_own(2)
+    keep = pltpu.make_async_copy(W.at[:, wrow(f, 0, 512), :], mas_hbm, own_sems.at[0])
+    keep.start()
+    moments_to(1)
+    ring_step(1)
+    w_partner(1)
+    moments_to(2)
+    w_relay(0, 0)
+    ring_step(2)
+    w_relay(2, 0)
+    w_relay(0, 1)
+    w_relay(1, 0)
+    moments_to(3)
+    ring_step(3)
+    w_relay(1, 1)
+    w_partner(2)
+
+    moments_to(4)
 
     side_arrived(7)
     side_arrived(1)
@@ -375,7 +386,7 @@
 
     first_ones = NDP * n_old // (n_old + n_new)
     grown_at = jnp.maximum(d - first_ones, 0) * 256
-    grown_scale = mask_ref[:, pl.ds(pl.multiple_of(grown_at, 256), 256)]
+    grown_scale = mask_ref[pl.ds(pl.multiple_of(grown_at, 256), 256)].reshape(1, 256)
     is_grown = jnp.where(d >= first_ones, 1.0, 0.0)
     scale = is_grown * grown_scale + (1.0 - is_grown)
 
@@ -421,7 +432,7 @@
     project(0, near, True)
     w_far(2, 0)
     send(wb(2, 2, 0), wb(2, 2, 0), w_recv.at[2, 7], YP)
-    moments_to(MOMENTS[1])
+    moments_to(5)
     project(1, near, True)
     w_far(0, 0)
     w_far(0, 1)
@@ -521,12 +532,13 @@
     core_sum(1)
     send(PT.at[zrows(4), left], RZp.at[0, :, left], rzp_recv.at[0], ZP)
     send(PT.at[zrows(4), right], RZm.at[0, :, right], rzm_recv.at[0], ZM)
-    moments_to(MOMENTS[2])
+    moments_to(6)
+    grad_gu(1, 1)
+    grad_gu(3, 1)
+    g_second(1, 1, 0, 512)
     core_sum(0)
     down_sum(2)
     g_first(2, 0, 512, 256)
-    grad_gu(1, 1)
-    grad_gu(3, 1)
 
     def z_step(s):
         whole = pl.ds(0, 4096)
@@ -540,41 +552,41 @@
             ).astype(BF)
             send(PT.at[zrows(k), :], got.at[s], sem.at[s], to)
 
-    g_second(1, 1, 0, 512)
     z_step(1)
-    moments_to(MOMENTS[3])
+    moments_to(7)
     grad_gu(1, 0)
     grad_gu(3, 0)
     g_second(0, 0, 0, 512)
     z_step(2)
-    moments_to(MOMENTS[4])
+    moments_to(8)
     down_sum(1)
     down_sum(3)
     g_second(2, 0, 512, 256)
     grad_gu(0, 1)
+
+    RYS[...] = g_third(1, 1, 0, 512).T.astype(BF)
+    send(RYS, RY, ry_recv.at[0], YP)
+    z_step(3)
+    moments_to(9)
     grad_gu(0, 0)
     down_sum(0)
-    z_step(3)
-    moments_to(MOMENTS[5])
-
-    G[0, 1, 0:512] = g_third(1, 1, 0, 512).astype(BF)
-    send(G.at[0, 1, pl.ds(0, 512), :], RY, ry_recv.at[0], YP)
 
     arrived(RZp.at[3], rzp_recv.at[3])
     arrived(RZm.at[3], rzm_recv.at[3])
     nearby = PT[zrows(0), :].astype(F32) + RZp[3].astype(F32) + RZm[3].astype(F32)
     PT[16:32, :] = nearby[16:].astype(BF)
     send(PT.at[pl.ds(16, 16), :], RYH, ryh_recv.at[0], YN)
-    moments_to(MOMENTS[6])
-
-    grad_ref[2] = g_third(2, 0, 512, 256).T
-    both = g_third(0, 0, 0, 512)
+    moments_to(10)
+
     arrived(RYH, ryh_recv.at[0])
     out_ref[...] = (nearby[:16] + RYH[...].astype(F32)).astype(BF)
-    arrived(RY, ry_recv.at[0])
-    both = both + RY[...].astype(F32)
+    both = g_third(0, 0, 0, 512)
     grad_ref[0] = both[:256].T
     grad_ref[1] = both[256:].T
+    arrived(RY, ry_recv.at[0])
+    for p in (0, 1):
+        grad_ref[p] = grad_ref[p] + RY[:, p * 256 : (p + 1) * 256].astype(F32)
+    grad_ref[2] = g_third(2, 0, 512, 256).T
 
     for half, dst in enumerate((fst_hbm, snd_hbm)):
         arrived(dst.at[:, pl.ds(0, 496), :], m_recv.at[half])
@@ -636,6 +648,7 @@
             pltpu.VMEM((2, 768, 512), BF),
             pltpu.VMEM((2, 768, 512), BF),
             pltpu.VMEM((512, 512), BF),
+            pltpu.VMEM((512, 512), BF),
             pltpu.VMEM((4, 256, 512), BF),
             pltpu.VMEM((2, 256, 4096), BF),
             pltpu.VMEM((256, 4096), BF),
@@ -668,7 +681,7 @@
             collective_id=0, has_side_effects=True, vmem_limit_bytes=64000 * 1024
         ),
         name="grown_step",
-    )(tokens, upstream, *planes, grow_mask.reshape(1, -1))
+    )(tokens, upstream, *planes, grow_mask)
     updated = adam_update(
         master.astype(F32), first.astype(F32), second.astype(F32), gradients
     )

time: 139 us -> 134 us (0.964)
  Pallas kernels: 131 us -> 126 us
    pallas_call x1, Pallas kernels: 131 us -> 126 us  [local(): pl.pallas_call(step_kernel, out_shape=(jax.ShapeDtypeStruct((16, 4096), B...]
where the time goes in v3:
time: 134 us; the launch traced here: 133 us
  Pallas kernels  126 us (94%)
  other arithmetic  5.55 us (4%)
    pallas_call x1, Pallas kernels, local(): pl.pallas_call(step_kernel, out_shape=(jax.ShapeDtypeStruct((16, 4096), B...  126 us
    transpose x1, other arithmetic, local(): return (out,) + tuple((jnp.transpose(a, (1, 0, 2)) for a in updated))  5.55 us

profile of v3, /device:TPU:1, one launch (start us, length us, event | category | flops | bytes accessed | tf_op | source)
XLA Modules:
  0.0 133.0 jit_solution(10911821280682416166)
XLA Ops:
  0.6 126.1 %grown_step.1 = (bf16[16,4096]{1,0:T(8,128)(2,1)}, f32[3,512,256]{2,1,0:T(8,128)}, bf16[3,512,256]{2,1,0:T(8,128)(2,1)}, bf16[3,512,256]{2,1,0:T(8,128)(2,1)}, bf16[3,512,256]{2,1,0:T(8,128)(2,1)}) custom-call(bf16[16,4096]{1,0:T(8,128)(2,1)} %tok_hbm.1, bf16[16,4096]{1,0:T(8,128)(2,1)} %ups_hbm.1, f32[3,16,5632]{2,1,0:T(8,128)} %bitcast.12, ...), custom_call_target="tpu_custom_call" | custom-call | tf_op jit(solution)/shard_map/grown_step/pallas_call | solution.py:625
  126.7 0.0 copy-start
  126.7 5.6 %fusion.5 = (f32[512,3,256]{2,0,1:T(8,128)}, f32[512,3,256]{2,0,1:T(8,128)}, f32[512,3,256]{2,0,1:T(8,128)}) fusion(f32[3,512,256]{2,1,0:T(8,128)} %get-tuple-element.12, bf16[3,512,256]{2,1,0:T(8,128)(2,1)} %get-tuple-element.13, bf16[3,512,256]{2,1,0:T(8,128)(2,1)} %get-tuple-element.11, bf16[3,512,256]{2,1,0:T(8,128)(2,1)} %get-tuple-element.10), kind=kLoop, calls=%fused_computation.9 | loop fusion | flops 6684672 | bytes 8650752 | tf_op jit(solution)/shard_map/transpose | solution.py:688
  132.3 0.0 copy-done
  132.3 0.7 copy.14
Async XLA Ops:
  126.7 5.6 %copy-start = (bf16[16,4096]{1,0:T(8,128)(2,1)S(1)}, bf16[16,4096]{1,0:T(8,128)(2,1)}, u32[]{:S(2)}) copy-start(bf16[16,4096]{1,0:T(8,128)(2,1)} %get-tuple-element.21) | copy-start | bytes 393220

commit v4 on v3

--- a/solution.py
+++ b/solution.py
@@ -23,6 +23,8 @@
 MOMENTS = (
     (0, 0), (0, 0), (0, 0), (0, 0), (15, 0), (15, 4), (15, 7), (15, 10), (15, 13), (15, 16), (15, 16),
 )
+Q = 0
+XF, YF = 512 + Q, 256 - Q
 PLACE = {k: i for i, k in enumerate((0, 1, 7, 2, 6, 3, 5, 4))}
 
 
@@ -350,11 +352,11 @@
     side_arrived(0)
     w_own(1)
     w_partner(0)
+    ring_step(1)
     w_own(2)
     keep = pltpu.make_async_copy(W.at[:, wrow(f, 0, 512), :], mas_hbm, own_sems.at[0])
     keep.start()
     moments_to(1)
-    ring_step(1)
     w_partner(1)
     moments_to(2)
     w_relay(0, 0)
@@ -457,10 +459,14 @@
         G[dx, du, 0:512] = jnp.dot(
             XT[0:512], tcols(0, fs(dx, du)), preferred_element_type=F32
         ).astype(BF)
+        if Q:
+            G[dx, du, 512:XF] = jnp.dot(
+                XT[512:XF], tcols(1, fs(dx, du)), preferred_element_type=F32
+            ).astype(BF)
 
     def grad_down(dx, du):
-        G[dx, du, 512:768] = jnp.dot(
-            XT[512:768], tcols(1, fs(dx, du)), preferred_element_type=F32
+        G[dx, du, XF:768] = jnp.dot(
+            XT[XF:768], tcols(1, fs(dx, du)), preferred_element_type=F32
         ).astype(BF)
 
     def out_part(v):
@@ -500,22 +506,22 @@
         )
 
     grad_gu(2, 1)
-    g_first(1, 1, 0, 512)
+    g_first(1, 1, 0, XF)
+    for dx in (2, 1, 3, 0):
+        grad_down(dx, 1)
+        send(G.at[dx, 1, pl.ds(XF, YF), :], RYF.at[dx], ryf_recv.at[dx], YP)
     grad_gu(2, 0)
-    g_first(0, 0, 0, 512)
+    g_first(0, 0, 0, XF)
     out_part(1)
     for h in (0, 1):
         rows = pl.ds(h * 128, 128)
         send(O.at[1, rows, :], RC.at[rows, :], rc_recv.at[h], CP)
-    for dx in (2, 1, 3, 0):
-        grad_down(dx, 1)
-        send(G.at[dx, 1, pl.ds(512, 256), :], RYF.at[dx], ryf_recv.at[dx], YP)
     out_part(0)
 
     def down_sum(dx):
         arrived(RYF.at[dx], ryf_recv.at[dx])
-        G[dx, 0, 512:768, :] = (
-            jnp.dot(XT[512:768], tcols(1, fs(dx, 0)), preferred_element_type=F32)
+        G[dx, 0, XF:768, :] = (
+            jnp.dot(XT[XF:768], tcols(1, fs(dx, 0)), preferred_element_type=F32)
             .astype(BF)
             .astype(F32)
             + RYF[dx].astype(F32)
@@ -535,10 +541,10 @@
     moments_to(6)
     grad_gu(1, 1)
     grad_gu(3, 1)
-    g_second(1, 1, 0, 512)
+    g_second(1, 1, 0, XF)
     core_sum(0)
     down_sum(2)
-    g_first(2, 0, 512, 256)
+    g_first(2, 0, XF, YF)
 
     def z_step(s):
         whole = pl.ds(0, 4096)
@@ -556,15 +562,15 @@
     moments_to(7)
     grad_gu(1, 0)
     grad_gu(3, 0)
-    g_second(0, 0, 0, 512)
+    g_second(0, 0, 0, XF)
     z_step(2)
     moments_to(8)
     down_sum(1)
     down_sum(3)
-    g_second(2, 0, 512, 256)
+    g_second(2, 0, XF, YF)
     grad_gu(0, 1)
 
-    RYS[...] = g_third(1, 1, 0, 512).T.astype(BF)
+    RYS[...] = g_third(1, 1, 0, XF).T.astype(BF)
     send(RYS, RY, ry_recv.at[0], YP)
     z_step(3)
     moments_to(9)
@@ -580,13 +586,17 @@
 
     arrived(RYH, ryh_recv.at[0])
     out_ref[...] = (nearby[:16] + RYH[...].astype(F32)).astype(BF)
-    both = g_third(0, 0, 0, 512)
+    both = g_third(0, 0, 0, XF)
     grad_ref[0] = both[:256].T
-    grad_ref[1] = both[256:].T
+    grad_ref[1] = both[256:512].T
+    if Q:
+        grad_ref[2, :, 0:Q] = both[512:].T
     arrived(RY, ry_recv.at[0])
     for p in (0, 1):
         grad_ref[p] = grad_ref[p] + RY[:, p * 256 : (p + 1) * 256].astype(F32)
-    grad_ref[2] = g_third(2, 0, 512, 256).T
+    if Q:
+        grad_ref[2, :, 0:Q] = grad_ref[2, :, 0:Q] + RY[:, 512:].astype(F32)
+    grad_ref[2, :, Q:] = g_third(2, 0, XF, YF).T
 
     for half, dst in enumerate((fst_hbm, snd_hbm)):
         arrived(dst.at[:, pl.ds(0, 496), :], m_recv.at[half])
@@ -647,9 +657,9 @@
             pltpu.VMEM((2, 768, 512), BF),
             pltpu.VMEM((2, 768, 512), BF),
             pltpu.VMEM((2, 768, 512), BF),
-            pltpu.VMEM((512, 512), BF),
-            pltpu.VMEM((512, 512), BF),
-            pltpu.VMEM((4, 256, 512), BF),
+            pltpu.VMEM((512, XF), BF),
+            pltpu.VMEM((512, XF), BF),
+            pltpu.VMEM((4, YF, 512), BF),
             pltpu.VMEM((2, 256, 4096), BF),
             pltpu.VMEM((256, 4096), BF),
             pltpu.VMEM((256, 4096), BF),

time: 134 us -> 133 us (level)
  no operation moved by 1% of the time
where the time goes in v4:
time: 133 us
  Pallas kernels  126 us (95%)
  other arithmetic  5.55 us (4%)
    pallas_call x1, Pallas kernels, local(): pl.pallas_call(step_kernel, out_shape=(jax.ShapeDtypeStruct((16, 4096), B...  126 us
    transpose x1, other arithmetic, local(): return (out,) + tuple((jnp.transpose(a, (1, 0, 2)) for a in updated))  5.55 us

profile of v4, /device:TPU:1, one launch (start us, length us, event | category | flops | bytes accessed | tf_op | source)
XLA Modules:
  0.0 132.6 jit_solution(17180818883194686927)
XLA Ops:
  0.6 125.8 %grown_step.1 = (bf16[16,4096]{1,0:T(8,128)(2,1)}, f32[3,512,256]{2,1,0:T(8,128)}, bf16[3,512,256]{2,1,0:T(8,128)(2,1)}, bf16[3,512,256]{2,1,0:T(8,128)(2,1)}, bf16[3,512,256]{2,1,0:T(8,128)(2,1)}) custom-call(bf16[16,4096]{1,0:T(8,128)(2,1)} %tok_hbm.1, bf16[16,4096]{1,0:T(8,128)(2,1)} %ups_hbm.1, f32[3,16,5632]{2,1,0:T(8,128)} %bitcast.12, ...), custom_call_target="tpu_custom_call" | custom-call | tf_op jit(solution)/shard_map/grown_step/pallas_call | solution.py:635
  126.4 0.0 copy-start
  126.4 5.6 %fusion.5 = (f32[512,3,256]{2,0,1:T(8,128)}, f32[512,3,256]{2,0,1:T(8,128)}, f32[512,3,256]{2,0,1:T(8,128)}) fusion(f32[3,512,256]{2,1,0:T(8,128)} %get-tuple-element.12, bf16[3,512,256]{2,1,0:T(8,128)(2,1)} %get-tuple-element.13, bf16[3,512,256]{2,1,0:T(8,128)(2,1)} %get-tuple-element.11, bf16[3,512,256]{2,1,0:T(8,128)(2,1)} %get-tuple-element.10), kind=kLoop, calls=%fused_computation.9 | loop fusion | flops 6684672 | bytes 8650752 | tf_op jit(solution)/shard_map/transpose | solution.py:698
  132.0 0.0 copy-done
  132.0 0.7 copy.14
Async XLA Ops:
  126.4 5.6 %copy-start = (bf16[16,4096]{1,0:T(8,128)(2,1)S(1)}, bf16[16,4096]{1,0:T(8,128)(2,1)}, u32[]{:S(2)}) copy-start(bf16[16,4096]{1,0:T(8,128)(2,1)} %get-tuple-element.21) | copy-start | bytes 393220
